TPU v7x, 256 devices: a whole 4x4x8 slice. The times are simulated.
256 devices in a mesh: ctx: 32 (over x_hi, z, core), head: 8 (over x_lo, y).
Axes of the slice: x: 4 (x_hi: 2, x_lo: 2; x = x_hi * 2 + x_lo), y: 4, z: 8, core: 2. Of those that a mesh axis runs over, the one named last changes fastest.
Arguments:
- queries: bfloat16 [6656, 4096], P('ctx', 'head'), may hold values from -4 to 4
- rotated_key_rows: bfloat16 [6656, 1024], P('ctx', 'head'), may hold values from -4 to 4
- value_matrix: bfloat16 [6656, 1024], P('ctx', 'head'), may hold values from -4 to 4
- out_grad: bfloat16 [6656, 4096], P('ctx', 'head'), may hold values from -6 to 6
- w_out: bfloat16 [4096, 4096], P('head'), may hold values from -0.09375 to 0.09375
- doc_lengths: int32 [16], replicated, may hold values from 1 to 3744, 6656 in all
Outputs:
- grad_q: bfloat16 [6656, 4096], P('ctx', 'head')
- key_gradient: bfloat16 [6656, 1024], P('ctx', 'head')
- value_gradient: bfloat16 [6656, 1024], P('ctx', 'head')
- grad_wo_t: bfloat16 [4096, 4096], P('ctx', 'head')
Inputs may be any that keep to these rules, and one draw needn't show every extreme that they name: `doc_lengths`: 16 lengths summing to 6656; the longest is exactly 3744.
All inputs are finite; a program needn't handle non-finite values.
Results may differ from a plain program's by a relative error of at most 0.019.
Values may be sent and summed in bfloat16 or wider, within the bound.
A program may use at most 128 MiB of HBM per device.

v0:
```python
import jax
import jax.numpy as jnp
from jax import lax
from jax.sharding import PartitionSpec as P

HEAD_SIZE = 128


def per_device(queries, rotated_key_rows, value_matrix, out_grad, w_out, doc_lengths):
    tok_rows = queries.shape[0]
    q_heads = queries.shape[1] // HEAD_SIZE
    kv_heads = rotated_key_rows.shape[1] // HEAD_SIZE
    query_group_width = q_heads // kv_heads
    key_width = kv_heads * HEAD_SIZE
    logit_scale = HEAD_SIZE ** (-0.5)
    ctx_count = lax.axis_size("ctx")
    total_rows = tok_rows * ctx_count
    my_first = lax.axis_index("ctx") * tok_rows
    hi_pos = my_first + tok_rows - 1
    doc_ends = jnp.cumsum(doc_lengths)
    my_positions = my_first + jnp.arange(tok_rows, dtype=jnp.int32)
    my_segs = jnp.sum(
        jnp.where(doc_ends[None, :] <= my_positions[:, None], doc_lengths[None, :], 0), axis=1
    )
    lo_seg = jnp.min(my_segs)
    q_tiles = queries.reshape(tok_rows, kv_heads, query_group_width, HEAD_SIZE)
    key_all, value_all = (
        lax.all_gather(rotated_key_rows, "ctx", axis=0, tiled=True),
        lax.all_gather(value_matrix, "ctx", axis=0, tiled=True),
    )
    grad_cols = lax.all_gather(out_grad, "head", axis=1, tiled=True)
    key_block = 512
    block_count = total_rows // key_block

    def masked(q_pos, q_seg, key_pos):
        allowed = (key_pos[None, :] <= q_pos[:, None]) & (key_pos[None, :] >= q_seg[:, None])
        return allowed[None, :, None, :]

    def key_slice(block_index):
        offset = block_index * key_block
        key_tile = lax.dynamic_slice_in_dim(key_all, offset, key_block, 0).reshape(
            key_block, kv_heads, HEAD_SIZE
        )
        value_tile = lax.dynamic_slice_in_dim(value_all, offset, key_block, 0).reshape(
            key_block, kv_heads, HEAD_SIZE
        )
        key_pos = offset + jnp.arange(key_block, dtype=jnp.int32)
        active = (offset <= hi_pos) & (offset + key_block - 1 >= lo_seg)
        return (offset, key_tile, value_tile, key_pos, active)

    def forward_step(block_index, loop_state):
        offset, key_tile, value_tile, key_pos, active = key_slice(block_index)
        weighted, totals = loop_state
        scores = (
            jnp.einsum("tgrd,kgd->gtrk", q_tiles, key_tile, preferred_element_type=jnp.float32)
            * logit_scale
        )
        expo_vals = jnp.where(masked(my_positions, my_segs, key_pos), jnp.exp(scores), 0.0)
        weighted = weighted + jnp.einsum(
            "gtrk,kgd->tgrd",
            expo_vals.astype(jnp.bfloat16),
            value_tile,
            preferred_element_type=jnp.float32,
        )
        return (weighted, totals + jnp.sum(expo_vals, axis=3))

    start_state = (
        jnp.zeros((tok_rows, kv_heads, query_group_width, HEAD_SIZE), jnp.float32),
        jnp.zeros((kv_heads, tok_rows, query_group_width), jnp.float32),
    )
    weighted, totals = lax.fori_loop(0, block_count, forward_step, start_state)
    attn_tiles = (weighted / jnp.transpose(totals, (1, 0, 2))[..., None]).astype(jnp.bfloat16)
    log_total = jnp.log(totals)
    attn_flat = attn_tiles.reshape(tok_rows, q_heads * HEAD_SIZE)
    grad_attn = lax.dot_general(
        grad_cols, w_out, (((1,), (1,)), ((), ())), preferred_element_type=jnp.float32
    ).astype(jnp.bfloat16)
    grad_tiles = grad_attn.reshape(tok_rows, kv_heads, query_group_width, HEAD_SIZE)
    row_delta = jnp.transpose(
        jnp.sum(grad_tiles.astype(jnp.float32) * attn_tiles.astype(jnp.float32), axis=3), (1, 0, 2)
    )

    def grad_tile(q_part, g_part, lt_part, rd_part, q_pos, q_seg, key_tile, value_tile, key_pos):
        allowed = masked(q_pos, q_seg, key_pos)
        scores = (
            jnp.einsum("tgrd,kgd->gtrk", q_part, key_tile, preferred_element_type=jnp.float32)
            * logit_scale
        )
        attn_weights = jnp.where(allowed, jnp.exp(scores - lt_part[..., None]), 0.0)
        grad_weights = jnp.einsum(
            "tgrd,kgd->gtrk", g_part, value_tile, preferred_element_type=jnp.float32
        )
        dscore = (attn_weights * (grad_weights - rd_part[..., None])).astype(jnp.bfloat16)
        dq_term = jnp.einsum("gtrk,kgd->tgrd", dscore, key_tile, preferred_element_type=jnp.float32)
        dk_term = jnp.einsum("gtrk,tgrd->kgd", dscore, q_part, preferred_element_type=jnp.float32)
        dv_term = jnp.einsum(
            "gtrk,tgrd->kgd",
            attn_weights.astype(jnp.bfloat16),
            g_part,
            preferred_element_type=jnp.float32,
        )
        return (dq_term, dk_term, dv_term)

    zero_q = jnp.zeros((tok_rows, kv_heads, query_group_width, HEAD_SIZE), jnp.float32)

    def backward_step(block_index, loop_state):
        offset, key_tile, value_tile, key_pos, active = key_slice(block_index)
        q_accum, kv_accum = loop_state
        dq_term, dk_term, dv_term = grad_tile(
            q_tiles,
            grad_tiles,
            log_total,
            row_delta,
            my_positions,
            my_segs,
            key_tile,
            value_tile,
            key_pos,
        )
        joined = jnp.concatenate(
            [dk_term.reshape(key_block, key_width), dv_term.reshape(key_block, key_width)], axis=1
        )
        return (q_accum + dq_term, lax.dynamic_update_slice_in_dim(kv_accum, joined, offset, 0))

    q_accum, kv_accum = lax.fori_loop(
        0, block_count, backward_step, (zero_q, jnp.zeros((total_rows, 2 * key_width), jnp.float32))
    )
    own_grads = lax.psum_scatter(
        kv_accum.astype(jnp.bfloat16), "ctx", scatter_dimension=0, tiled=True
    ).astype(jnp.float32)
    key_gradient = (logit_scale * own_grads[:, :key_width]).astype(jnp.bfloat16)
    value_gradient = own_grads[:, key_width:].astype(jnp.bfloat16)
    grad_wo = lax.psum_scatter(
        lax.dot_general(
            grad_cols, attn_flat, (((0,), (0,)), ((), ())), preferred_element_type=jnp.float32
        ).astype(jnp.bfloat16),
        "ctx",
        scatter_dimension=0,
        tiled=True,
    )
    grad_q = (logit_scale * q_accum).reshape(tok_rows, q_heads * HEAD_SIZE).astype(jnp.bfloat16)
    return (grad_q, key_gradient, value_gradient, grad_wo)


def solution(mesh):
    return jax.shard_map(
        per_device,
        mesh=mesh,
        in_specs=(
            P("ctx", "head"),
            P("ctx", "head"),
            P("ctx", "head"),
            P("ctx", "head"),
            P("head", None),
            P(),
        ),
        out_specs=(P("ctx", "head"), P("ctx", "head"), P("ctx", "head"), P("ctx", "head")),
        check_vma=False,
    )
```

profile of v0, /device:TPU:8, one launch (start us, length us, event | category | flops | bytes accessed | tf_op | source)
XLA Modules:
  0.0 594.3 jit_solution(7932197649029800151)
XLA Ops:
  12.1 41.0 %all-gather.8.cloned.1.call-done = bf16[208,4096]{1,0:T(8,128)(2,1)} async-done(((bf16[208,512]{1,0:T(8,128)(2,1)}), bf16[208,4096]{1,0:T(8,128)(2,1)}) %all-gather.8.cloned.1.call-update) | async-done | bytes 1703952 | tf_op jit(solution)/shard_map/all_gather | solution.py:31
  53.2 4.2 convolution_convert_fusion.1
  57.5 79.3 %all-gather.4.cloned.1.call-done = bf16[6656,128]{1,0:T(8,128)(2,1)} async-done(((bf16[208,128]{1,0:T(8,128)(2,1)}), bf16[6656,128]{1,0:T(8,128)(2,1)}) %all-gather.4.cloned.1.call-update) | async-done | bytes 1703952 | tf_op jit(solution)/shard_map/all_gather | solution.py:28
  136.8 78.0 %all-gather.6.cloned.1.call-done = bf16[6656,128]{1,0:T(8,128)(2,1)} async-done(((bf16[208,128]{1,0:T(8,128)(2,1)}), bf16[6656,128]{1,0:T(8,128)(2,1)}) %all-gather.6.cloned.1.call-update) | async-done | bytes 1703952 | tf_op jit(solution)/shard_map/all_gather | solution.py:29
  214.9 41.1 %while.32 = (s32[]{:T(128)}, f32[208,1,4,128]{3,0,2,1:T(8,128)S(1)}, f32[1,208,4]{1,2,0:T(4,128)S(1)}, bf16[6656,128]{1,0:T(8,128)(2,1)}, s32[208]{0:T(256)S(1)}...) while((s32[]{:T(128)}, ...), condition=%wide.region_4.5_spmd.clone, body=%wide.region_2.4_spmd.clone.sunk | while | flops 220341792 | bytes 3264134 | solution.py:71
  215.0 1.6 fusion.57
  218.2 1.6 fusion.57
  221.4 1.6 fusion.57
  224.5 1.6 fusion.57
  227.7 1.6 fusion.57
  230.8 1.6 fusion.57
  234.0 1.6 fusion.57
  237.2 1.6 fusion.57
  240.3 1.6 fusion.57
  243.5 1.6 fusion.57
  246.7 1.6 fusion.57
  249.8 1.6 fusion.57
  253.0 1.6 fusion.57
  256.3 2.0 broadcast_in_dim.86.clone
  258.4 76.8 %while.33 = (s32[]{:T(128)}, f32[208,1,4,128]{3,0,2,1:T(8,128)S(1)}, bf16[6656,256]{1,0:T(8,128)(2,1)}, bf16[6656,128]{1,0:T(8,128)(2,1)}, s32[208]{0:T(256)S(1)...) while((s32[]{:T(128)}, ...), condition=%wide.region_7.8_spmd.clone, body=%wide.region_6.7_spmd.clone.sunk | while | flops 549298944 | bytes 11826341 | solution.py:125
  264.5 1.5 bitcast_select_fusion.3
  270.4 1.5 bitcast_select_fusion.3
  282.2 1.5 bitcast_select_fusion.3
  288.1 1.5 bitcast_select_fusion.3
  299.9 1.5 bitcast_select_fusion.3
  311.8 1.5 bitcast_select_fusion.3
  317.7 1.5 bitcast_select_fusion.3
  323.6 1.5 bitcast_select_fusion.3
  336.7 3.3 fusion.29
  339.9 6.5 %copy.43 = bf16[4096,512]{1,0:T(8,128)(2,1)} copy(bf16[4096,512]{0,1:T(8,128)(2,1)} %fusion.29) | data formatting | bytes 8388608
  347.3 109.5 %reduce-scatter.5.cloned.1.call-done = bf16[208,256]{1,0:T(8,128)(2,1)} async-done(((bf16[6656,256]{1,0:T(8,128)(2,1)}), bf16[208,256]{1,0:T(8,128)(2,1)}) %reduce-scatter.5.cloned.1.call-update) | async-done | bytes 106512 | tf_op jit(solution)/shard_map/reduce_scatter | solution.py:128
  459.7 128.1 %reduce-scatter.7.cloned.1.call-done = bf16[128,512]{1,0:T(8,128)(2,1)} async-done(((bf16[4096,512]{1,0:T(8,128)(2,1)}), bf16[128,512]{1,0:T(8,128)(2,1)}) %reduce-scatter.7.cloned.1.call-update) | async-done | bytes 131088
  (232 shorter events, 94.8 us)
Async XLA Ops:
  7.2 46.0 %all-gather.8.cloned.1.call-start = ((), (), s32[]{:S(2)}) async-start(), calls=%async_computation.4 | async-start | bytes 1916928 | tf_op jit(solution)/shard_map/all_gather | solution.py:31
  7.9 128.9 %all-gather.4.cloned.1.call-start = ((), (), s32[]{:S(2)}) async-start(), calls=%async_computation.2 | async-start | bytes 1757184 | tf_op jit(solution)/shard_map/all_gather | solution.py:28
  8.6 206.2 %all-gather.6.cloned.1.call-start = ((), (), s32[]{:S(2)}) async-start(), calls=%async_computation.3 | async-start | bytes 1757184 | tf_op jit(solution)/shard_map/all_gather | solution.py:29
  9.4 447.5 %reduce-scatter.5.cloned.1.call-start = ((), (), s32[]{:S(2)}) async-start(), calls=%async_computation.5 | async-start | bytes 3514368 | tf_op jit(solution)/shard_map/reduce_scatter | solution.py:128
  335.2 1.5 copy-start
  335.3 252.6 %reduce-scatter.7.cloned.1.call-start = ((), (), s32[]{:S(2)}) async-start(), calls=%async_computation.6 | async-start | bytes 4325376
Sparse Core Ops, SparseCore 0:
  9.8 43.3 all-gather.7
  55.9 80.9 all-gather.3
  139.5 75.2 all-gather.5
  335.4 121.4 reduce-scatter.4
  461.5 126.2 reduce-scatter.6
where the time goes:
time: 596 us; the launch traced here: 594 us
  waiting for transfers between devices  438 us (73%)
  matrix products  108 us (18%)
  local copies, waits for them, and re-layouts  25.2 us (4%)
  between operations  13.9 us (2%)
  other arithmetic  7.38 us (1%)
    unnamed x6, waiting for transfers between devices  130 us
    reduce_scatter x1, waiting for transfers between devices, per_device(): lax.psum_scatter(kv_accum.astype(jnp.bfloat16), 'ctx', scatter_dimension=...  110 us
    all_gather x1, waiting for transfers between devices, per_device(): lax.all_gather(rotated_key_rows, 'ctx', axis=0, tiled=True)  79.3 us
    all_gather x1, waiting for transfers between devices, per_device(): lax.all_gather(value_matrix, 'ctx', axis=0, tiled=True)  78 us
    all_gather x1, waiting for transfers between devices, per_device(): grad_cols = lax.all_gather(out_grad, 'head', axis=1, tiled=True)  41 us
    dot_general x13, matrix products, forward_step(): jnp.einsum('tgrd,kgd->gtrk', q_tiles, key_tile, preferred_element_type=jn...  20.5 us
    dot_general x13, matrix products, grad_tile(): jnp.einsum('tgrd,kgd->gtrk', q_part, key_tile, preferred_element_type=jnp...  18.9 us
    dot_general x13, matrix products, grad_tile(): jnp.einsum('gtrk,kgd->tgrd', dscore, key_tile, preferred_element_type=jnp...  17.7 us
  transfers between devices with their start and end apart: 5, of which 5 were waited for; matrix products, arithmetic and copies ran while one was open for 3% of the time, Pallas kernels for 0%

commit v1 on v0

--- a/solution.py
+++ b/solution.py
@@ -4,6 +4,13 @@
 from jax.sharding import PartitionSpec as P
 
 HEAD_SIZE = 128
+
+
+def gather_over(x, mesh_axis, along):
+    size = lax.axis_size(mesh_axis)
+    shards = jnp.stack([x for _ in range(size)])
+    shards = lax.all_to_all(shards, mesh_axis, split_axis=0, concat_axis=0)
+    return jnp.concatenate(shards, axis=along)
 
 
 def per_device(queries, rotated_key_rows, value_matrix, out_grad, w_out, doc_lengths):
@@ -25,7 +32,7 @@
     lo_seg = jnp.min(my_segs)
     q_tiles = queries.reshape(tok_rows, kv_heads, query_group_width, HEAD_SIZE)
     key_all, value_all = (
-        lax.all_gather(rotated_key_rows, "ctx", axis=0, tiled=True),
+        gather_over(rotated_key_rows, "ctx", 0),
         lax.all_gather(value_matrix, "ctx", axis=0, tiled=True),
     )
     grad_cols = lax.all_gather(out_grad, "head", axis=1, tiled=True)

time: 596 us -> 494 us (0.83)
  waiting for transfers between devices: 438 us -> 360 us
  matrix products: 108 us -> 72.8 us
  starting transfers between devices: 0.19 us -> 11.6 us
    all_gather x1 -> x0, waiting for transfers between devices: 79.3 us -> none  [per_device(): lax.all_gather(rotated_key_rows, 'ctx', axis=0, tiled=True)]
    dot_general x13, matrix products: 18.9 us -> 7.12 us  [grad_tile(): jnp.einsum('tgrd,kgd->gtrk', q_part, key_tile, preferred_element_type=jnp...]
    dot_general x13, matrix products: 20.5 us -> 8.77 us  [forward_step(): jnp.einsum('tgrd,kgd->gtrk', q_tiles, key_tile, preferred_element_type=jn...]
    dot_general x13, matrix products: 17.7 us -> 5.97 us  [grad_tile(): jnp.einsum('gtrk,kgd->tgrd', dscore, key_tile, preferred_element_type=jnp...]
    all_to_all x0 -> x1, starting transfers between devices: none -> 11.4 us  [gather_over(): shards = lax.all_to_all(shards, mesh_axis, split_axis=0, concat_axis=0)]
    all_gather x1, waiting for transfers between devices: 78 us -> 84.5 us  [per_device(): lax.all_gather(value_matrix, 'ctx', axis=0, tiled=True)]
    unnamed x6 -> x5, waiting for transfers between devices: 130 us -> 130 us
  transfers between devices with their start and end apart: 5 -> 5, of which waited for: 5 -> 4; matrix products, arithmetic and copies ran while one was open for 3% -> 4% of each run, Pallas kernels for 0% -> 0%
where the time goes in v1:
time: 494 us; the launch traced here: 493 us
  waiting for transfers between devices  360 us (73%)
  matrix products  72.8 us (15%)
  local copies, waits for them, and re-layouts  26 us (5%)
  between operations  13.9 us (3%)
  starting transfers between devices  11.6 us (2%)
  other arithmetic  6.73 us (1%)
    unnamed x5, waiting for transfers between devices  130 us
    reduce_scatter x1, waiting for transfers between devices, per_device(): lax.psum_scatter(kv_accum.astype(jnp.bfloat16), 'ctx', scatter_dimension=...  110 us
    all_gather x1, waiting for transfers between devices, per_device(): lax.all_gather(value_matrix, 'ctx', axis=0, tiled=True)  84.5 us
    all_gather x1, waiting for transfers between devices, per_device(): grad_cols = lax.all_gather(out_grad, 'head', axis=1, tiled=True)  36.4 us
    dot_general x13, matrix products, forward_step(): jnp.einsum('gtrk,kgd->tgrd', expo_vals.astype(jnp.bfloat16), value_tile,...  17.7 us
    dot_general x13, matrix products, grad_tile(): jnp.einsum('tgrd,kgd->gtrk', g_part, value_tile, preferred_element_type=j...  16.9 us
    all_to_all x1, starting transfers between devices, gather_over(): shards = lax.all_to_all(shards, mesh_axis, split_axis=0, concat_axis=0)  11.4 us
    dynamic_update_slice x26, local copies, waits for them, and re-layouts, backward_step(): lax.dynamic_update_slice_in_dim(kv_accum, joined, offset, 0)  11.3 us
  transfers between devices with their start and end apart: 5, of which 4 were waited for; matrix products, arithmetic and copies ran while one was open for 4% of the time, Pallas kernels for 0%

profile of v1, /device:TPU:8, one launch (start us, length us, event | category | flops | bytes accessed | tf_op | source)
XLA Modules:
  0.0 492.7 jit_solution(12420677244109417904)
XLA Ops:
  8.6 2.2 stack.2
  10.9 11.4 %all-to-all-start = ((bf16[32,208,128]{2,1,0:T(8,128)(2,1)}), bf16[32,208,128]{2,1,0:T(8,128)(2,1)S(1)}, u32[]{:S(2)}, u32[]{:S(2)}) async-start(bf16[32,208,128]{2,1,0:T(8,128)(2,1)} %stack.2), calls=%async_computation | async-start | bytes 3407872 | tf_op jit(solution)/shard_map/all_to_all | solution.py:12
  22.9 36.4 %all-gather.5.cloned.1.call-done = bf16[208,4096]{1,0:T(8,128)(2,1)} async-done(((bf16[208,512]{1,0:T(8,128)(2,1)}), bf16[208,4096]{1,0:T(8,128)(2,1)}) %all-gather.5.cloned.1.call-update) | async-done | bytes 1703952 | tf_op jit(solution)/shard_map/all_gather | solution.py:38
  59.3 4.2 convolution_convert_fusion.1
  63.6 84.5 %all-gather.3.cloned.1.call-done = bf16[6656,128]{1,0:T(8,128)(2,1)} async-done(((bf16[208,128]{1,0:T(8,128)(2,1)}), bf16[6656,128]{1,0:T(8,128)(2,1)}) %all-gather.3.cloned.1.call-update) | async-done | bytes 1703952 | tf_op jit(solution)/shard_map/all_gather | solution.py:36
  148.1 29.4 %while.32 = (s32[]{:T(128)}, f32[208,1,4,128]{3,0,2,1:T(8,128)S(1)}, f32[1,208,4]{1,2,0:T(4,128)S(1)}, bf16[6656,128]{1,0:T(8,128)(2,1)}, s32[208]{0:T(256)S(1)}...) while((s32[]{:T(128)}, ...), condition=%wide.region_4.5_spmd.clone, body=%wide.region_2.4_spmd.clone.sunk | while | flops 220341792 | bytes 3264134 | solution.py:78
  149.0 1.4 fusion.58
  151.2 1.4 fusion.58
  153.5 1.4 fusion.58
  155.8 1.4 fusion.58
  158.0 1.4 fusion.58
  160.3 1.4 fusion.58
  162.6 1.4 fusion.58
  164.8 1.4 fusion.58
  167.1 1.4 fusion.58
  169.4 1.4 fusion.58
  171.6 1.4 fusion.58
  173.9 1.4 fusion.58
  176.2 1.4 fusion.58
  178.0 2.1 broadcast_in_dim.86.clone
  180.0 53.4 %while.33 = (s32[]{:T(128)}, f32[208,1,4,128]{3,0,2,1:T(8,128)S(1)}, bf16[6656,256]{1,0:T(8,128)(2,1)}, bf16[6656,128]{1,0:T(8,128)(2,1)S(1)}, s32[208]{0:T(256)...) while((s32[]{:T(128)}, ...), condition=%wide.region_7.8_spmd.clone, body=%wide.region_6.7_spmd.clone.sunk | while | flops 549298944 | bytes 11827109 | solution.py:132
  181.1 1.3 fusion.69
  189.3 1.3 fusion.69
  201.6 1.3 fusion.69
  205.7 1.3 fusion.69
  213.9 1.3 fusion.69
  234.9 3.3 fusion.29
  238.1 6.5 %copy.43 = bf16[4096,512]{1,0:T(8,128)(2,1)} copy(bf16[4096,512]{0,1:T(8,128)(2,1)} %fusion.29) | data formatting | bytes 8388608
  245.5 109.6 %reduce-scatter.5.cloned.1.call-done = bf16[208,256]{1,0:T(8,128)(2,1)} async-done(((bf16[6656,256]{1,0:T(8,128)(2,1)}), bf16[208,256]{1,0:T(8,128)(2,1)}) %reduce-scatter.5.cloned.1.call-update) | async-done | bytes 106512 | tf_op jit(solution)/shard_map/reduce_scatter | solution.py:135
  355.1 1.4 slice.14
  356.5 1.4 multiply_convert_fusion.1
  358.0 128.2 %reduce-scatter.7.cloned.1.call-done = bf16[128,512]{1,0:T(8,128)(2,1)} async-done(((bf16[4096,512]{1,0:T(8,128)(2,1)}), bf16[128,512]{1,0:T(8,128)(2,1)}) %reduce-scatter.7.cloned.1.call-update) | async-done | bytes 131088
  (236 shorter events, 61.8 us)
Async XLA Ops:
  7.2 52.1 %all-gather.5.cloned.1.call-start = ((), (), s32[]{:S(2)}) async-start(), calls=%async_computation.4 | async-start | bytes 1916928 | tf_op jit(solution)/shard_map/all_gather | solution.py:38
  7.9 140.2 %all-gather.3.cloned.1.call-start = ((), (), s32[]{:S(2)}) async-start(), calls=%async_computation.3 | async-start | bytes 1757184 | tf_op jit(solution)/shard_map/all_gather | solution.py:36
  10.9 11.5 %copy-start.2 = (s32[16]{0:T(128)S(1)}, s32[16]{0:T(128)}, u32[]{:S(2)}) copy-start(s32[16]{0:T(128)} %param.15) | copy-start | bytes 196
  10.9 11.8 %copy-start.1 = (bf16[208,512]{1,0:T(8,128)(2,1)S(1)}, bf16[208,512]{1,0:T(8,128)(2,1)}, u32[]{:S(2)}) copy-start(bf16[208,512]{1,0:T(8,128)(2,1)} %param.10) | copy-start | bytes 638980
  10.9 137.2 %all-to-all-start = ((bf16[32,208,128]{2,1,0:T(8,128)(2,1)}), bf16[32,208,128]{2,1,0:T(8,128)(2,1)S(1)}, u32[]{:S(2)}, u32[]{:S(2)}) async-start(bf16[32,208,128]{2,1,0:T(8,128)(2,1)} %stack.2), calls=%async_computation | async-start | bytes 3407872 | tf_op jit(solution)/shard_map/all_to_all | solution.py:12
  22.3 332.7 %reduce-scatter.5.cloned.1.call-start = ((), (), s32[]{:S(2)}) async-start(), calls=%async_computation.5 | async-start | bytes 3514368 | tf_op jit(solution)/shard_map/reduce_scatter | solution.py:135
  233.4 1.5 copy-start
  233.4 252.7 %reduce-scatter.7.cloned.1.call-start = ((), (), s32[]{:S(2)}) async-start(), calls=%async_computation.6 | async-start | bytes 4325376
Sparse Core Ops, SparseCore 0:
  9.8 49.4 all-gather.4
  61.9 86.1 all-gather.2
  233.6 121.4 reduce-scatter.4
  359.7 126.3 reduce-scatter.6
